TPU v7x, 256 devices: a whole 4x4x8 slice. The times are simulated.
256 devices in a mesh: col: 64 (over y, z, core), row: 4 (over x).
Axes of the slice: x: 4, y: 4, z: 8, core: 2. Of those that a mesh axis runs over, the one named last changes fastest.
Arguments:
- tile_left: bfloat16 [64, 8, 1024, 64], P('col', 'row'), may hold values from -0.41992188 to 0.41992188
- tile_right: bfloat16 [64, 8, 1024, 64], P('col', 'row'), may hold values from -0.1875 to 0.1875
- row_left: bfloat16 [64, 1024, 64], P('col'), may hold values from -0.41992188 to 0.41992188
- row_right: bfloat16 [64, 1024, 64], P('col'), may hold values from -0.1875 to 0.1875
- sketch: bfloat16 [1024, 64], replicated, may hold values from -6 to 6
- panel_left: bfloat16 [8, 1024, 64], P('row'), may hold values from -0.375 to 0.375
- panel_right: bfloat16 [8, 1024, 64], P('row'), may hold values from -0.1875 to 0.1875
- pivot_inverse: bfloat16 [1024, 1024], replicated, as said below
- band_inverse: bfloat16 [8, 1024, 1024], P('row'), as said below
- link_left: bfloat16 [8, 1024, 64], P('row'), may hold values from -0.75 to 0.75
- link_right: bfloat16 [8, 1024, 64], P('row'), may hold values from -0.0625 to 0.0625
- pivot_rhs: bfloat16 [1024, 32768], P(None, 'col'), may hold values from -6 to 6
- band_rhs: bfloat16 [8, 1024, 32768], P('row', None, 'col'), may hold values from -6 to 6
- carry_in: float32 [64, 32768], P(None, 'col'), may hold values from -3 to 3
Outputs:
- pivot_solution: bfloat16 [1024, 32768], P(None, 'col')
- schur_right: float32 [8, 1024, 64], P('row', 'col')
- band_solution: bfloat16 [8, 1024, 32768], P('row', None, 'col')
- link_states: float32 [8, 64, 32768], P('row', None, 'col')
Inputs may be any that keep to these rules, and one draw needn't show every extreme that they name: `pivot_inverse`: each tile is lower triangular with a positive diagonal, the inverse of a Cholesky factor of a diagonal covariance tile. `band_inverse`: each tile is lower triangular with a positive diagonal, the inverse of a Cholesky factor of a diagonal covariance tile.
All inputs are finite; a program needn't handle non-finite values.
Results may differ from a plain program's by a relative error of at most 0.0056.
Values sent between devices are 32-bit elements; how exact they have to be, the bound alone decides.
A program may use at most 128 MiB of HBM per device.

v0:
```python
import jax
import jax.numpy as jnp
from jax import lax
from jax.sharding import PartitionSpec as P

HIGHEST_PRECISION = lax.Precision.HIGHEST


def from_behind(block, axis, distance):
    devices = range(lax.axis_size(axis))
    route = [(i - distance, i) for i in devices if i - distance in devices]
    return lax.ppermute(block, axis, route)


def widened(array):
    return array.astype(jnp.float32)


def lower_inverse(gram_matrix):
    gram_lower = jnp.linalg.cholesky(gram_matrix)
    identity_matrix = jnp.broadcast_to(
        jnp.eye(gram_matrix.shape[-1], dtype=jnp.float32), gram_matrix.shape
    )
    return lax.linalg.triangular_solve(gram_lower, identity_matrix, left_side=True, lower=True)


def shards(
    tile_left,
    tile_right,
    row_left,
    row_right,
    sketch,
    panel_left,
    panel_right,
    pivot_inverse,
    band_inverse,
    link_left,
    link_right,
    pivot_rhs,
    band_rhs,
    carry_in,
):
    pivot_solution = jnp.dot(pivot_inverse, pivot_rhs, preferred_element_type=jnp.float32).astype(
        jnp.bfloat16
    )
    pulled = jnp.einsum(
        "nm,nc->mc", pivot_inverse, pivot_solution, preferred_element_type=jnp.float32
    )
    coupling = jnp.einsum(
        "jbnr,jns->jbrs", tile_right, row_right, preferred_element_type=jnp.float32
    )
    probe_core = jnp.einsum("jnr,ns->jrs", row_left, sketch, preferred_element_type=jnp.float32)
    sketch_core = jnp.einsum("jbrs,jst->jbrt", coupling, probe_core, precision=HIGHEST_PRECISION)
    left_wide = widened(tile_left)
    sketch_terms = jnp.einsum("jbnr,jbrt->bnt", left_wide, sketch_core, precision=HIGHEST_PRECISION)
    sketched = lax.psum(sketch_terms, "col")
    gram_matrix = jnp.einsum("bnr,bns->brs", sketched, sketched, precision=HIGHEST_PRECISION)
    inverse_low = lower_inverse(gram_matrix)
    panel_basis = jnp.einsum("bnr,bsr->bns", sketched, inverse_low, precision=HIGHEST_PRECISION)
    projected = jnp.einsum("jbnr,bns->jbrs", left_wide, panel_basis, precision=HIGHEST_PRECISION)
    middle = jnp.einsum("jbrs,jbrt->jbst", coupling, projected, precision=HIGHEST_PRECISION)
    schur_terms = jnp.einsum(
        "jns,jbst->bnt", widened(row_left), middle, precision=HIGHEST_PRECISION
    )
    schur_full = lax.psum(schur_terms, "col")
    slab_rows = schur_full.shape[1] // lax.axis_size("col")
    schur_right = lax.dynamic_slice_in_dim(
        schur_full, lax.axis_index("col") * slab_rows, slab_rows, 1
    )
    panel_coeffs = jnp.einsum(
        "bnr,nc->brc", widened(panel_right), pulled, precision=HIGHEST_PRECISION
    )
    schur_coeffs = jnp.einsum("bnr,nc->brc", schur_full, pulled, precision=HIGHEST_PRECISION)
    panel_term = jnp.einsum(
        "bnr,brc->bnc", widened(panel_left), panel_coeffs, precision=HIGHEST_PRECISION
    ) - jnp.einsum("bnr,brc->bnc", panel_basis, schur_coeffs, precision=HIGHEST_PRECISION)
    reduced = (band_rhs.astype(jnp.float32) - panel_term).astype(jnp.bfloat16)
    local_part = jnp.einsum(
        "bnm,bmc->bnc", band_inverse, reduced, preferred_element_type=jnp.float32
    )
    feed_columns = jnp.einsum(
        "bnm,bmr->bnr", band_inverse, link_left, preferred_element_type=jnp.float32
    )
    right_wide = widened(link_right)
    band_count = band_rhs.shape[0]
    leading = lax.axis_index("row") == 0

    def last_state(prior_state):
        for position in range(band_count):
            solved = local_part[position] - jnp.dot(
                feed_columns[position], prior_state, precision=HIGHEST_PRECISION
            )
            prior_state = jnp.einsum(
                "nr,nc->rc", right_wide[position], solved, precision=HIGHEST_PRECISION
            )
        return prior_state

    def relay_section(section_index, incoming_state):
        shifted = from_behind(last_state(incoming_state), "row", 1)
        return jnp.where(leading, carry_in, shifted)

    incoming = lax.fori_loop(0, lax.axis_size("row") - 1, relay_section, carry_in)
    solved_rows = []
    state_rows = []
    prior_state = incoming
    for position in range(band_count):
        solved = local_part[position] - jnp.dot(
            feed_columns[position], prior_state, precision=HIGHEST_PRECISION
        )
        prior_state = jnp.einsum(
            "nr,nc->rc", right_wide[position], solved, precision=HIGHEST_PRECISION
        )
        solved_rows.append(solved.astype(jnp.bfloat16))
        state_rows.append(prior_state)
    return (pivot_solution, schur_right, jnp.stack(solved_rows), jnp.stack(state_rows))


def solution(mesh):
    return jax.shard_map(
        shards,
        mesh=mesh,
        in_specs=(
            P("col", "row", None, None),
            P("col", "row", None, None),
            P("col", None, None),
            P("col", None, None),
            P(),
            P("row", None, None),
            P("row", None, None),
            P(),
            P("row", None, None),
            P("row", None, None),
            P("row", None, None),
            P(None, "col"),
            P("row", None, "col"),
            P(None, "col"),
        ),
        out_specs=(
            P(None, "col"),
            P("row", "col", None),
            P("row", None, "col"),
            P("row", None, "col"),
        ),
        check_vma=False,
    )
```

profile of v0, /device:TPU:1, one launch (start us, length us, event | category | flops | bytes accessed | tf_op | source)
XLA Modules:
  0.0 509.3 jit_solution(8060935407227560381)
XLA Ops:
  10.1 2.1 convolution_bitcast_fusion.2
  15.1 4.4 fusion.48
  19.5 2.5 copy.31
  21.9 2.5 convolution_convert_fusion
  25.4 2.6 fusion.46
  28.0 169.4 %all-reduce.3.cloned.1.call-done = f32[2,1024,64]{1,2,0:T(8,128)} async-done(((f32[2,1024,64]{1,2,0:T(8,128)}), f32[2,1024,64]{1,2,0:T(8,128)}) %all-reduce.3.cloned.1.call-update) | async-done | bytes 524304 | tf_op jit(solution)/shard_map/psum | solution.py:56
  201.4 12.5 %custom-call.7 = f32[2,64,64]{2,1,0:T(8,128)S(1)} custom-call(f32[2,64,64]{2,1,0:T(8,128)} %fusion.39), custom_call_target="Cholesky" | custom-call | tf_op jit(solution)/shard_map/jit(cholesky)/cholesky | solution.py:20
  214.7 10.7 %custom-call.8 = f32[2,1,64,64]{2,3,1,0:T(8,128)S(1)} custom-call(f32[2,1,64,64]{3,2,1,0:T(8,128)} %select_bitcast_fusion), custom_call_target="InvertDiagBlocksLowerTriangular" | custom-call | tf_op jit(solution)/shard_map/triangular_solve | solution.py:24
  231.7 3.6 fusion.22
  235.3 2.0 copy.36
  237.3 175.0 %all-reduce.5.cloned.1.call-done = f32[2,1024,64]{1,2,0:T(8,128)} async-done(((f32[2,1024,64]{1,2,0:T(8,128)}), f32[2,1024,64]{1,2,0:T(8,128)}) %all-reduce.5.cloned.1.call-update) | async-done | bytes 524304 | tf_op jit(solution)/shard_map/psum | solution.py:65
  412.3 4.1 fusion.20
  416.4 3.5 fusion.47
  420.0 2.3 fusion.17
  422.3 5.1 convolution_bitcast_fusion
  427.3 5.4 %copy.30 = f32[2,1024,512]{2,1,0:T(8,128)} copy(f32[2,1024,512]{1,2,0:T(8,128)} %convolution_bitcast_fusion) | data formatting | bytes 8388608 | tf_op jit(solution)/shard_map/while | solution.py:102
  432.8 51.3 %while.10 = (s32[]{:T(128)}, f32[64,512]{1,0:T(8,128)S(1)}, pred[]{:T(512)}, f32[2,1024,512]{2,1,0:T(8,128)}, f32[2,1024,64]{2,1,0:T(8,128)}, /*index=5*/f32[2,1...) while((s32[]{:T(128)}, f32[64,512]{1,0:T(8,128)S(1)}, pred[]{:T(512)}, f32[2,1024,512]{2,1,0:T(8,128)}, ...), condition=%wide.region_5.6_spmd, body=%wide.region_4.5_spmd.sunk | while | flops 1611694080 | bytes 35127476 | solution.py:102
  432.8 2.9 fusion.96
  435.7 5.2 %fusion.97 = f32[512,64]{1,0:T(8,128)S(1)} fusion(f32[1024,512]{1,0:T(8,128)S(1)} %fusion.96, f32[2,1024,512]{2,1,0:T(8,128)} %get-tuple-element.142, f32[2,1024,64]{2,1,0:T(8,128)S(1)} %get-tuple-element.144), kind=kOutput, calls=%fused_computation.3.clone.1 | convolution fusion | flops 403177472 | bytes 4849664 | tf_op jit(solution)/shard_map/while/body/eval_jaxpr/nr,nc->rc/dot_general | solution.py:93
  444.3 3.1 collective-permute-start
  447.4 1.9 collective-permute-done
  449.3 2.9 fusion.96
  452.3 5.2 %fusion.97 = f32[512,64]{1,0:T(8,128)S(1)} fusion(f32[1024,512]{1,0:T(8,128)S(1)} %fusion.96, f32[2,1024,512]{2,1,0:T(8,128)} %get-tuple-element.142, f32[2,1024,64]{2,1,0:T(8,128)S(1)} %get-tuple-element.144), kind=kOutput, calls=%fused_computation.3.clone.1 | convolution fusion | flops 403177472 | bytes 4849664 | tf_op jit(solution)/shard_map/while/body/eval_jaxpr/nr,nc->rc/dot_general | solution.py:93
  460.8 3.8 collective-permute-start
  464.6 1.9 collective-permute-done
  466.6 2.9 fusion.96
  469.5 5.2 %fusion.97 = f32[512,64]{1,0:T(8,128)S(1)} fusion(f32[1024,512]{1,0:T(8,128)S(1)} %fusion.96, f32[2,1024,512]{2,1,0:T(8,128)} %get-tuple-element.142, f32[2,1024,64]{2,1,0:T(8,128)S(1)} %get-tuple-element.144), kind=kOutput, calls=%fused_computation.3.clone.1 | convolution fusion | flops 403177472 | bytes 4849664 | tf_op jit(solution)/shard_map/while/body/eval_jaxpr/nr,nc->rc/dot_general | solution.py:93
  478.1 3.8 collective-permute-start
  481.9 1.9 collective-permute-done
  484.1 3.7 fusion.19
  495.1 2.7 pad_maximum_fusion
  497.8 3.9 copy.35
  (80 shorter events, 35.7 us)
Async XLA Ops:
  7.2 14.8 %copy-start = (bf16[1024,1024]{1,0:T(8,128)(2,1)S(1)}, bf16[1024,1024]{1,0:T(8,128)(2,1)}, u32[]{:S(2)}) copy-start(bf16[1024,1024]{1,0:T(8,128)(2,1)} %param.23) | copy-start | bytes 6291460
  7.2 5.7 %copy-start.7 = (f32[64,512]{1,0:T(8,128)S(1)}, f32[64,512]{1,0:T(8,128)}, u32[]{:S(2)}) copy-start(f32[64,512]{1,0:T(8,128)} %param.29) | copy-start | bytes 393220
  7.2 5.7 %copy-start.12 = (bf16[2,1024,64]{1,2,0:T(8,128)(2,1)S(1)}, bf16[2,1024,64]{1,2,0:T(8,128)(2,1)}, u32[]{:S(2)}) copy-start(bf16[2,1024,64]{1,2,0:T(8,128)(2,1)} %param.26) | copy-start | bytes 786436
  7.2 190.2 %all-reduce.3.cloned.1.call-start = ((), (), s32[]{:S(2)}) async-start(), calls=%async_computation | async-start | bytes 1048576 | tf_op jit(solution)/shard_map/psum | solution.py:56
  12.2 400.1 %all-reduce.5.cloned.1.call-start = ((), (), s32[]{:S(2)}) async-start(), calls=%async_computation.1 | async-start | bytes 1048576 | tf_op jit(solution)/shard_map/psum | solution.py:65
  24.4 1.0 copy-start.11
  225.5 5.1 copy-start.14
  228.2 0.8 copy-start.5
  412.3 4.1 copy-start.6
  416.4 3.6 copy-start.9
  416.4 3.6 copy-start.10
  416.4 3.6 copy-start.15
  420.0 2.3 copy-start.8
  432.8 8.2 %copy-start.2 = (f32[2,1024,64]{2,1,0:T(8,128)S(1)}, f32[2,1024,64]{2,1,0:T(8,128)}, u32[]{:S(2)}) copy-start(f32[2,1024,64]{2,1,0:T(8,128)} %get-tuple-element.143) | copy-start | bytes 1572868 | tf_op jit(solution)/shard_map/while
  435.7 7.1 %copy-start.1 = (f32[2,1024,512]{2,1,0:T(8,128)S(1)}, f32[2,1024,512]{2,1,0:T(8,128)}, u32[]{:S(2)}) copy-start(f32[2,1024,512]{2,1,0:T(8,128)} %get-tuple-element.142) | copy-start | bytes 12582916 | tf_op jit(solution)/shard_map/while
  444.3 5.0 collective-permute-start
  449.3 8.2 %copy-start.2 = (f32[2,1024,64]{2,1,0:T(8,128)S(1)}, f32[2,1024,64]{2,1,0:T(8,128)}, u32[]{:S(2)}) copy-start(f32[2,1024,64]{2,1,0:T(8,128)} %get-tuple-element.143) | copy-start | bytes 1572868 | tf_op jit(solution)/shard_map/while
  452.3 7.1 %copy-start.1 = (f32[2,1024,512]{2,1,0:T(8,128)S(1)}, f32[2,1024,512]{2,1,0:T(8,128)}, u32[]{:S(2)}) copy-start(f32[2,1024,512]{2,1,0:T(8,128)} %get-tuple-element.142) | copy-start | bytes 12582916 | tf_op jit(solution)/shard_map/while
  460.8 5.7 %collective-permute-start = (f32[64,512]{1,0:T(8,128)S(1)}, f32[64,512]{1,0:T(8,128)S(1)}, u32[]{:S(2)}, u32[]{:S(2)}) collective-permute-start(f32[64,512]{1,0:T(8,128)S(1)} %fusion.99), channel_id=1, source_target_pairs={{0,1},{1,2},{2,3},{4,5},{5,6},{6,7},{8,9},{9,10},{10,11},{12,13},{... | collective-permute-start | bytes 393224 | tf_op jit(solution)/shard_map/while/body/eval_jaxpr/ppermute | solution.py:12
  466.6 8.2 %copy-start.2 = (f32[2,1024,64]{2,1,0:T(8,128)S(1)}, f32[2,1024,64]{2,1,0:T(8,128)}, u32[]{:S(2)}) copy-start(f32[2,1024,64]{2,1,0:T(8,128)} %get-tuple-element.143) | copy-start | bytes 1572868 | tf_op jit(solution)/shard_map/while
  469.5 7.1 %copy-start.1 = (f32[2,1024,512]{2,1,0:T(8,128)S(1)}, f32[2,1024,512]{2,1,0:T(8,128)}, u32[]{:S(2)}) copy-start(f32[2,1024,512]{2,1,0:T(8,128)} %get-tuple-element.142) | copy-start | bytes 12582916 | tf_op jit(solution)/shard_map/while
  478.1 5.7 %collective-permute-start = (f32[64,512]{1,0:T(8,128)S(1)}, f32[64,512]{1,0:T(8,128)S(1)}, u32[]{:S(2)}, u32[]{:S(2)}) collective-permute-start(f32[64,512]{1,0:T(8,128)S(1)} %fusion.99), channel_id=1, source_target_pairs={{0,1},{1,2},{2,3},{4,5},{5,6},{6,7},{8,9},{9,10},{10,11},{12,13},{... | collective-permute-start | bytes 393224 | tf_op jit(solution)/shard_map/while/body/eval_jaxpr/ppermute | solution.py:12
  484.1 3.7 copy-start.13
  484.1 5.0 copy-start.3
  487.8 1.2 copy-start.4
Sparse Core Ops, SparseCore 0:
  12.3 185.0 all-reduce.2
  231.9 180.3 all-reduce.4
where the time goes:
time: 516 us; the launch traced here: 509 us
  waiting for transfers between devices  350 us (68%)
  matrix products  82.4 us (16%)
  other arithmetic  32.1 us (6%)
  local copies, waits for them, and re-layouts  19 us (4%)
  between operations  14.4 us (3%)
  starting transfers between devices  10.7 us (2%)
    psum x1, waiting for transfers between devices, shards(): schur_full = lax.psum(schur_terms, 'col')  175 us
    psum x1, waiting for transfers between devices, shards(): sketched = lax.psum(sketch_terms, 'col')  169 us
    dot_general x6, matrix products, last_state(): jnp.einsum('nr,nc->rc', right_wide[position], solved, precision=HIGHEST_P...  20 us
    dot_general x6, matrix products, last_state(): jnp.dot(feed_columns[position], prior_state, precision=HIGHEST_PRECISION)  14.3 us
    another operation x4, other arithmetic, lower_inverse(): gram_lower = jnp.linalg.cholesky(gram_matrix)  12.6 us
    another operation x3, other arithmetic, lower_inverse(): lax.linalg.triangular_solve(gram_lower, identity_matrix, left_side=True,...  11.5 us
    ppermute x3, starting transfers between devices, from_behind(): return lax.ppermute(block, axis, route)  10.7 us
  transfers between devices with their start and end apart: 5, of which 5 were waited for; matrix products, arithmetic and copies ran while one was open for 4% of the time, Pallas kernels for 0%

commit v1 on v0

v1 whole, which is shorter than its diff:
```python
import jax
import jax.numpy as jnp
from jax import lax
from jax.experimental import pallas as pl
from jax.experimental.pallas import tpu as pltpu
from jax.sharding import PartitionSpec as P

F32 = jnp.float32
BF16 = jnp.bfloat16
HIGHEST = lax.Precision.HIGHEST
MESH = pl.DeviceIdType.MESH
NY, NZ, NX = 4, 8, 4
BLK = 256


def nn(a, b):
    return jnp.dot(a, b, preferred_element_type=F32)


def nt(a, b):
    return lax.dot_general(a, b, (((1,), (1,)), ((), ())), preferred_element_type=F32)


def tn(a, b):
    return lax.dot_general(a, b, (((0,), (0,)), ((), ())), preferred_element_type=F32)


def nn_full(a, b):
    return jnp.dot(a, b, precision=HIGHEST, preferred_element_type=F32)


def nt_full(a, b):
    return lax.dot_general(
        a, b, (((1,), (1,)), ((), ())), precision=HIGHEST, preferred_element_type=F32
    )


def high_low(a):
    high = a.astype(BF16)
    return high, (a - high.astype(F32)).astype(BF16)


def stacked_parts(a):
    return jnp.concatenate(high_low(a), axis=0)


def joined_rows(a):
    half = a.shape[0] // 2
    return a[:half] + a[half:]


def distance(k):
    return 4 + lax.div(k + 1, 2) * (1 - 2 * lax.rem(k, 2))


def kernel(
    tl_h, tr_h, rl_h, rr_h, sk_h, pl_h, pr_h, pi_h, bi_h, ll_h, lr_h, prhs_h, brhs_h, carry_h,
    ps_o, sr_o, bs_o, ls_o,
    tl, tr, rl, rr, sk, plt, prt, pi, bi, ll, lr, prhs, red, carry,
    ps, pulled, rl2, coup, vhl, pchl, l0, ms, a0, xx, sol, states, srout,
    terms1, core1, sum1, yin1, ysum1, zin1, full1,
    terms2, core2, sum2, yin2, ysum2, zin2, full2, zfull,
    yfull, yhl, qhl, chol, bt, es,
    xa_own, xn_own, xa, xn, xz_own, xz, cps, early,
    load_sem, out_sem,
    c_send, c_recv, y_send, y_recv, z_send, z_recv,
    gz_send, gz_recv, gy_send, gy_recv, gc_send, gc_recv,
    x_send, x_recv,
):
    me = lax.axis_index("col")
    x = lax.axis_index("row")
    c = lax.rem(me, 2)
    z = lax.rem(lax.div(me, 2), NZ)
    y = lax.div(me, 2 * NZ)

    def at_core():
        return {"col": (y * NZ + z) * 2 + (1 - c)}

    def at_y(dy):
        return {"col": (lax.rem(y + dy, NY) * NZ + z) * 2 + c}

    def at_z(d):
        return {"col": (y * NZ + lax.rem(z + d, NZ)) * 2 + c}

    def at_x(d):
        return {"row": lax.rem(x + d, NX)}

    loads = [
        pltpu.make_async_copy(src, dst, load_sem.at[i])
        for i, (src, dst) in enumerate(
            [
                (tr_h, tr), (rr_h, rr), (sk_h, sk), (rl_h, rl), (tl_h, tl),
                (pi_h, pi), (prhs_h, prhs), (lr_h, lr), (bi_h, bi), (ll_h, ll),
                (pr_h, prt), (pl_h, plt), (brhs_h, red), (carry_h, carry),
            ]
        )
    ]
    for i in range(5):
        loads[i].start()

    barrier = pltpu.get_barrier_semaphore()
    peers = [at_core()]
    peers += [at_y(d) for d in range(1, NY)]
    peers += [at_z(d) for d in range(1, NZ)]
    peers += [at_x(d) for d in range(1, NX)]
    for peer in peers:
        pl.semaphore_signal(barrier, inc=1, device_id=peer, device_id_type=MESH)

    def remote(src, dst, send, recv, device):
        return pltpu.make_async_remote_copy(
            src_ref=src, dst_ref=dst, send_sem=send, recv_sem=recv,
            device_id=device, device_id_type=MESH,
        )

    def reduce_scatter(s, terms, core, total, yin, ysum, zin):
        def core_copy(k):
            zt = lax.rem(z + distance(k), NZ)
            return remote(
                terms.at[(1 - c) * NZ + zt], core.at[zt], c_send.at[s, k], c_recv.at[s, k], at_core()
            )

        def y_copy(k, dy):
            zt = lax.rem(z + distance(k), NZ)
            return remote(
                total.at[zt, lax.rem(y + dy, NY)], yin.at[k, dy - 1],
                y_send.at[s, k, dy - 1], y_recv.at[s, k, dy - 1], at_y(dy),
            )

        def z_copy(k):
            return remote(
                ysum.at[k], zin.at[k], z_send.at[s, k], z_recv.at[s, k], at_z(distance(k))
            )

        def send_core():
            def step(k, carried):
                core_copy(k).start()
                return carried

            lax.fori_loop(0, NZ, step, 0)

        def fold_core():
            def step(k, carried):
                core_copy(k).wait_recv()
                zt = lax.rem(z + distance(k), NZ)
                total[zt] = terms[c * NZ + zt] + core[zt]
                for dy in range(1, NY):
                    y_copy(k, dy).start()
                return carried

            lax.fori_loop(0, NZ, step, 0)

        def y_total(k):
            for dy in range(1, NY):
                y_copy(k, dy).wait_recv()
            zt = lax.rem(z + distance(k), NZ)
            return (total[zt, y] + yin[k, 0]) + (yin[k, 1] + yin[k, 2])

        def fold_y():
            def step(k, carried):
                ysum[k] = y_total(k)
                z_copy(k).start()
                return carried

            lax.fori_loop(0, NZ - 1, step, 0)
            ysum[NZ - 1] = y_total(NZ - 1)

        def fold_z():
            block = ysum[NZ - 1]
            for k in range(NZ - 2, -1, -1):
                z_copy(k).wait_recv()
                block = block + zin[k]
            return block

        def finish():
            def step(k, carried):
                core_copy(k).wait_send()
                for dy in range(1, NY):
                    y_copy(k, dy).wait_send()
                return carried

            lax.fori_loop(0, NZ, step, 0)

            def step_z(k, carried):
                z_copy(k).wait_send()
                return carried

            lax.fori_loop(0, NZ - 1, step_z, 0)

        return send_core, fold_core, fold_y, fold_z, finish

    def all_gather(s, full):
        def z_copy(k):
            own = full.at[c * NZ + z, y]
            return remote(own, own, gz_send.at[s, k], gz_recv.at[s, k], at_z(distance(k)))

        def origin(k):
            return lax.rem(z - distance(k) + NZ, NZ)

        def z_arrival(k):
            block = full.at[c * NZ + origin(k), y]
            return remote(block, block, gz_send.at[s, k], gz_recv.at[s, k], at_z(distance(k)))

        def y_copy(k, dy):
            block = full.at[c * NZ + origin(k), y]
            return remote(
                block, block, gy_send.at[s, k, dy - 1], gy_recv.at[s, k, dy - 1], at_y(dy)
            )

        def y_arrival(k, dy):
            block = full.at[c * NZ + origin(k), lax.rem(y - dy + NY, NY)]
            return remote(
                block, block, gy_send.at[s, k, dy - 1], gy_recv.at[s, k, dy - 1], at_y(dy)
            )

        def core_copy(k):
            group = full.at[c * NZ + origin(k)]
            return remote(group, group, gc_send.at[s, k], gc_recv.at[s, k], at_core())

        def core_arrival(k):
            group = full.at[(1 - c) * NZ + origin(k)]
            return remote(group, group, gc_send.at[s, k], gc_recv.at[s, k], at_core())

        def send_z():
            def step(k, carried):
                z_copy(k).start()
                return carried

            lax.fori_loop(0, NZ - 1, step, 0)
            for dy in range(1, NY):
                y_copy(NZ - 1, dy).start()

        def pass_y():
            def step(i, carried):
                k = NZ - 2 - i
                z_arrival(k).wait_recv()
                for dy in range(1, NY):
                    y_copy(k, dy).start()
                return carried

            lax.fori_loop(0, NZ - 1, step, 0)

        def pass_core():
            def step(i, carried):
                k = NZ - 1 - i
                for dy in range(1, NY):
                    y_arrival(k, dy).wait_recv()
                core_copy(k).start()
                return carried

            lax.fori_loop(0, NZ, step, 0)

        def arrive():
            def step(i, carried):
                core_arrival(NZ - 1 - i).wait_recv()
                return carried

            lax.fori_loop(0, NZ, step, 0)

        def finish():
            def step(k, carried):
                for dy in range(1, NY):
                    y_copy(k, dy).wait_send()
                core_copy(k).wait_send()
                return carried

            lax.fori_loop(0, NZ, step, 0)

            def step_z(k, carried):
                z_copy(k).wait_send()
                return carried

            lax.fori_loop(0, NZ - 1, step_z, 0)

        return send_z, pass_y, pass_core, arrive, finish

    def x_copy(kind, d):
        src = (xa_own, xn_own, xz_own)[kind]
        dst = (xa, xn, xz)[kind].at[d - 1]
        return remote(src, dst, x_send.at[kind, d - 1], x_recv.at[kind, d - 1], at_x(d))

    rs1 = reduce_scatter(0, terms1, core1, sum1, yin1, ysum1, zin1)
    ag1 = all_gather(0, full1)
    rs2 = reduce_scatter(1, terms2, core2, sum2, yin2, ysum2, zin2)
    ag2 = all_gather(1, full2)
    ag3 = all_gather(2, zfull)

    def pivot_rows(m):
        top = (m + 1) * BLK
        block = nn(pi[m * BLK : top, :top], prhs[:top, :])
        ps[m * BLK : top, :] = block.astype(BF16)

    def pulled_rows(m):
        low, top = m * BLK, (m + 1) * BLK
        pulled[low:top, :] = tn(pi[low:, low:top], ps[low:, :]).astype(BF16)

    def link_inverse(b, m):
        low, top = m * BLK, (m + 1) * BLK
        block = nn(lr[b * 64 : (b + 1) * 64, low:], bi[b, low:, low:top])
        vhl[b, :, low:top] = stacked_parts(block)

    def panel_coeffs():
        coeffs = nn(prt[...], pulled[...])
        for b in range(2):
            pchl[b] = stacked_parts(coeffs[b * 64 : (b + 1) * 64])

    def reduce_rows(b, m):
        low, top = m * BLK, (m + 1) * BLK
        left = plt[b * 64 : (b + 1) * 64, low:top]
        term = tn(jnp.concatenate([left, left], axis=0), pchl[b])
        red[b, low:top, :] = (red[b, low:top, :].astype(F32) - term).astype(BF16)

    def local_rows(b, m):
        low, top = m * BLK, (m + 1) * BLK
        l0[b, low:top, :] = nn(bi[b, low:top, :top], red[b, :top, :])

    def chain_terms():
        for b in range(2):
            ms[b] = joined_rows(nt(vhl[b], ll[b * 64 : (b + 1) * 64, :]))
            a0[b] = joined_rows(nn(vhl[b], red[b]))
        through = nn_full(ms[1], ms[0])
        xn_own[...] = through
        first = jnp.where(x == 0, 1.0, 0.0).astype(F32)
        xa_own[...] = (
            a0[1] - nn_full(ms[1], a0[0]) + first * nn_full(through, carry[...])
        )
        for d in range(1, NX):
            x_copy(1, d).start()
            x_copy(0, d).start()

    def chain_start():
        for d in range(1, NX):
            x_copy(1, d).wait_recv()
            x_copy(0, d).wait_recv()
        flag = [jnp.where(x >= d, 1.0, 0.0).astype(F32) for d in range(NX)]
        two = flag[2] * xn[0]
        three = flag[3] * nn_full(xn[0], xn[1])
        cps[0, :64, :] = two
        cps[1, :64, :] = three
        cps[0, 64:, :] = jnp.zeros((64, 64), F32)
        cps[1, 64:, :] = jnp.zeros((64, 64), F32)
        early[...] = (
            (1.0 - flag[1]) * carry[...]
            + flag[1] * xa[0]
            + nn_full(two, xa[1])
            + nn_full(three, xa[2])
        )

    rows_i = lax.broadcasted_iota(jnp.int32, (128, 128), 0)
    cols_i = lax.broadcasted_iota(jnp.int32, (128, 128), 1)

    def gram():
        blocks = [yhl[b] for b in range(2)]
        for b in range(2):
            high, low = blocks[b][:64], blocks[b][64:]
            square = nt(high, high) + (nt(high, low) + nt(low, high))
            eye = jnp.where(
                lax.broadcasted_iota(jnp.int32, (64, 64), 0)
                == lax.broadcasted_iota(jnp.int32, (64, 64), 1),
                1.0,
                0.0,
            ).astype(F32)
            pair = [square, eye] if b == 0 else [eye, square]
            chol[b * 64 : (b + 1) * 64, :] = jnp.concatenate(pair, axis=1)

    def eliminate(first, last):
        work = [chol[b * 64 : (b + 1) * 64, :] for b in range(2)]
        done = [[], []]
        start = (first // 8) * 8
        for b in range(2):
            done[b] = work[b][:start]
            work[b] = work[b][start:]
        height = 64 - start
        row_id = lax.broadcasted_iota(jnp.int32, (height, 1), 0) + start
        for k in range(first, last):
            for b in range(2):
                lane = k + 64 * b
                body = work[b]
                pivot_row = body[k - start : k - start + 1, :]
                pivot = pivot_row[:, lane : lane + 1]
                column = body[:, lane : lane + 1]
                factor = jnp.where(row_id > k, column / pivot, 0.0)
                work[b] = body - factor * pivot_row
        for b in range(2):
            chol[b * 64 + start : (b + 1) * 64, :] = work[b]

    def factors():
        full = chol[...]
        pivots = jnp.sum(jnp.where(rows_i == cols_i, full, 0.0), axis=1, keepdims=True)
        scaled = full * lax.rsqrt(pivots)
        moved = pltpu.roll(scaled, 64, 1)
        same = (rows_i < 64) == (cols_i < 64)
        inverse = jnp.where(same, moved, 0.0)
        bt[:128, :] = inverse
        yt = jnp.concatenate([yfull[0], yfull[1]], axis=0)
        basis = nn_full(inverse, yt)
        for b in range(2):
            qhl[b] = stacked_parts(basis[b * 64 : (b + 1) * 64])
        pieces = []
        for b in range(2):
            cross = joined_rows(nt(vhl[b], qhl[b]))
            cross = cross + pltpu.roll(cross, 64, 1)
            es[b] = cross[:, :64]
        pieces = [-nn_full(ms[1], es[0]), es[1]]
        outward = nn_full(jnp.concatenate(pieces, axis=1), inverse)
        bt[128:192, :] = outward
        bt[192:, :] = jnp.zeros((64, 128), F32)

    def response_rows(b, m):
        low, top = m * BLK, (m + 1) * BLK
        right = jnp.concatenate(
            [qhl[b, :64, :top], ll[b * 64 : (b + 1) * 64, :top]], axis=0
        )
        xx[b, low:top, :] = nt(bi[b, low:top, :top], right).astype(BF16)

    for i in range(4):
        loads[i].wait()
    for i in range(5, 14):
        loads[i].start()
    coupling_t = nt(rr[...], tr[...])
    probe_t = nt(sk[...], rl[...])
    coup[...] = nt(tr[...], rr[...])
    core_t = nn_full(probe_t, coupling_t)
    loads[4].wait()
    for b in range(2):
        own = tl[b * 64 : (b + 1) * 64, :]
        parts = jnp.concatenate(high_low(core_t[:, b * 64 : (b + 1) * 64]), axis=1)
        block = nn(parts, jnp.concatenate([own, own], axis=0))
        for t in range(8):
            terms1[2 * t + b] = block[:, t * 128 : (t + 1) * 128].reshape(4, 16, 128)
    pl.semaphore_wait(barrier, len(peers))
    rs1[0]()
    wide = rl[...].astype(F32)
    rl2[...] = jnp.concatenate([wide, wide], axis=0).T.astype(BF16)
    rs1[1]()
    loads[5].wait()
    loads[6].wait()
    for m in range(4):
        pivot_rows(m)
    ps_out = pltpu.make_async_copy(ps, ps_o, out_sem.at[0])
    ps_out.start()
    rs1[2]()
    for m in range(4):
        pulled_rows(m)
    loads[10].wait()
    panel_coeffs()
    full1[c * NZ + z, y] = rs1[3]()
    ag1[0]()
    loads[7].wait()
    loads[8].wait()
    for b in range(2):
        for m in range(4):
            link_inverse(b, m)
    loads[11].wait()
    loads[12].wait()
    for b in range(2):
        for m in range(4):
            reduce_rows(b, m)
    ag1[1]()
    loads[9].wait()
    loads[13].wait()
    chain_terms()
    local_rows(0, 0)
    local_rows(0, 1)
    ag1[2]()
    local_rows(0, 2)
    ag1[3]()

    for b in range(2):
        yt = jnp.concatenate([full1[2 * t + b].reshape(64, 128) for t in range(8)], axis=1)
        yfull[b] = yt
        yhl[b] = stacked_parts(yt)
    middles = []
    for b in range(2):
        projected_t = joined_rows(nt(yhl[b], tl[b * 64 : (b + 1) * 64, :]))
        middles.append(nn_full(projected_t, coup[b * 64 : (b + 1) * 64, :]))
    middle_t = jnp.concatenate(middles, axis=0)
    terms2[...] = nt(rl2[...], jnp.concatenate(high_low(middle_t), axis=1)).reshape(16, 4, 16, 128)
    rs2[0]()
    gram()
    rs2[1]()
    for first in range(0, 32, 8):
        eliminate(first, first + 8)
    rs2[2]()
    for first in range(32, 64, 8):
        eliminate(first, first + 8)
    factors()
    chain_start()
    shard = nt_full(rs2[3](), bt[...])
    full2[c * NZ + z, y] = shard[:, :128]
    xz_own[...] = shard[:, 128:]
    for d in range(1, NX):
        x_copy(2, d).start()
    ag2[0]()
    local_rows(0, 3)
    for d in range(1, NX):
        x_copy(2, d).wait_recv()
    near = jnp.where(x >= 1, 1.0, 0.0).astype(F32)
    zfull[c * NZ + z, y] = (
        near * xz[0] + nt_full(xz[1][:, :64], cps[0]) + nt_full(xz[2][:, :64], cps[1])
    )
    ag3[0]()
    ag2[1]()
    local_rows(1, 0)
    local_rows(1, 1)
    ag3[1]()
    local_rows(1, 2)
    local_rows(1, 3)
    ag2[2]()
    for m in range(4):
        response_rows(0, m)
    ag3[2]()
    for m in range(4):
        response_rows(1, m)
    ag2[3]()
    ag3[3]()

    gathered = full2[...].reshape(1024, 128).astype(BF16)
    onward = zfull[...].reshape(1024, 128).astype(BF16)
    coeffs = tn(gathered, pulled[...])
    shift = tn(onward, pulled[...])
    mine = full2[lax.div(me, 4), lax.rem(me, 4)]
    srout[0] = mine[:, :64]
    srout[1] = mine[:, 64:]
    sr_out = pltpu.make_async_copy(srout, sr_o, out_sem.at[1])
    sr_out.start()
    prior = early[...] + shift[:64]
    bs_out = []
    for b in range(2):
        own = coeffs[b * 64 : (b + 1) * 64]
        state = a0[b] + nn_full(es[b], own) - nn_full(ms[b], prior)
        states[b] = state
        right = jnp.concatenate([own, -prior], axis=0).astype(BF16)
        for m in range(4):
            low, top = m * BLK, (m + 1) * BLK
            sol[b, low:top, :] = (l0[b, low:top, :] + nn(xx[b, low:top, :], right)).astype(BF16)
            copy = pltpu.make_async_copy(
                sol.at[b, pl.ds(low, BLK)], bs_o.at[b, pl.ds(low, BLK)], out_sem.at[3 + 4 * b + m]
            )
            copy.start()
            bs_out.append(copy)
        prior = state
    ls_out = pltpu.make_async_copy(states, ls_o, out_sem.at[2])
    ls_out.start()

    for phase in (rs1, ag1, rs2, ag2, ag3):
        phase[4]()
    for kind in range(3):
        for d in range(1, NX):
            x_copy(kind, d).wait_send()
    ps_out.wait()
    sr_out.wait()
    ls_out.wait()
    for copy in bs_out:
        copy.wait()


def flipped(array):
    return jnp.swapaxes(array, -1, -2)


def shards(
    tile_left, tile_right, row_left, row_right, sketch, panel_left, panel_right,
    pivot_inverse, band_inverse, link_left, link_right, pivot_rhs, band_rhs, carry_in,
):
    args = (
        flipped(tile_left).reshape(128, 1024),
        flipped(tile_right).reshape(128, 1024),
        flipped(row_left).reshape(64, 1024),
        flipped(row_right).reshape(64, 1024),
        flipped(sketch),
        flipped(panel_left).reshape(128, 1024),
        flipped(panel_right).reshape(128, 1024),
        pivot_inverse,
        band_inverse,
        flipped(link_left).reshape(128, 1024),
        flipped(link_right).reshape(128, 1024),
        pivot_rhs,
        band_rhs,
        carry_in,
    )
    vm = pltpu.VMEM
    comm = (16, 4, 16, 128)

    def comm_scratch():
        return [
            vm(comm, F32), vm((8, 4, 16, 128), F32), vm((8, 4, 16, 128), F32),
            vm((8, 3, 16, 128), F32), vm((8, 16, 128), F32), vm((7, 16, 128), F32), vm(comm, F32),
        ]

    scratch = [
        vm((128, 1024), BF16), vm((128, 1024), BF16), vm((64, 1024), BF16), vm((64, 1024), BF16),
        vm((64, 1024), BF16), vm((128, 1024), BF16), vm((128, 1024), BF16), vm((1024, 1024), BF16),
        vm((2, 1024, 1024), BF16), vm((128, 1024), BF16), vm((128, 1024), BF16),
        vm((1024, 512), BF16), vm((2, 1024, 512), BF16), vm((64, 512), F32),
        vm((1024, 512), BF16), vm((1024, 512), BF16), vm((1024, 128), BF16), vm((128, 64), F32),
        vm((2, 128, 1024), BF16), vm((2, 128, 512), BF16), vm((2, 1024, 512), F32),
        vm((2, 64, 64), F32), vm((2, 64, 512), F32), vm((2, 1024, 128), BF16),
        vm((2, 1024, 512), BF16), vm((2, 64, 512), F32), vm((2, 16, 64), F32),
        *comm_scratch(),
        *comm_scratch(), vm(comm, F32),
        vm((2, 64, 1024), F32), vm((2, 128, 1024), BF16), vm((2, 128, 1024), BF16),
        vm((128, 128), F32), vm((256, 128), F32), vm((2, 64, 64), F32),
        vm((64, 512), F32), vm((64, 64), F32), vm((3, 64, 512), F32), vm((3, 64, 64), F32),
        vm((16, 128), F32), vm((3, 16, 128), F32), vm((2, 128, 64), F32), vm((64, 512), F32),
    ]
    dma = pltpu.SemaphoreType.DMA
    sems = [
        dma((14,)), dma((11,)),
        dma((2, 8)), dma((2, 8)), dma((2, 8, 3)), dma((2, 8, 3)), dma((2, 7)), dma((2, 7)),
        dma((3, 7)), dma((3, 7)), dma((3, 8, 3)), dma((3, 8, 3)), dma((3, 8)), dma((3, 8)),
        dma((3, 3)), dma((3, 3)),
    ]
    anywhere = pl.BlockSpec(memory_space=pl.ANY)
    return pl.pallas_call(
        kernel,
        out_shape=(
            jax.ShapeDtypeStruct((1024, 512), BF16),
            jax.ShapeDtypeStruct((2, 16, 64), F32),
            jax.ShapeDtypeStruct((2, 1024, 512), BF16),
            jax.ShapeDtypeStruct((2, 64, 512), F32),
        ),
        in_specs=[anywhere] * 14,
        out_specs=(anywhere,) * 4,
        scratch_shapes=scratch + sems,
        compiler_params=pltpu.CompilerParams(
            collective_id=0, has_side_effects=True, vmem_limit_bytes=60 * 1024 * 1024
        ),
        name="panel_update",
    )(*args)


def solution(mesh):
    return jax.shard_map(
        shards,
        mesh=mesh,
        in_specs=(
            P("col", "row", None, None),
            P("col", "row", None, None),
            P("col", None, None),
            P("col", None, None),
            P(),
            P("row", None, None),
            P("row", None, None),
            P(),
            P("row", None, None),
            P("row", None, None),
            P("row", None, None),
            P(None, "col"),
            P("row", None, "col"),
            P(None, "col"),
        ),
        out_specs=(
            P(None, "col"),
            P("row", "col", None),
            P("row", None, "col"),
            P("row", None, "col"),
        ),
        check_vma=False,
    )
```

time: 516 us -> 66.7 us (0.13); the launches traced: 509 us -> 66.5 us
  waiting for transfers between devices: 350 us -> 0 us
  matrix products: 82.4 us -> 0 us
  Pallas kernels: 0 us -> 60.1 us
  other arithmetic: 32.1 us -> 0 us
  between operations: 14.4 us -> 0.66 us
  local copies, waits for them, and re-layouts: 19 us -> 5.76 us
  starting transfers between devices: 10.7 us -> 0 us
    psum x2 -> x0, waiting for transfers between devices: 344 us -> none  [the longest x1 175 us: shards(): schur_full = lax.psum(schur_terms, 'col')]
    dot_general x33 -> x0, matrix products: 81.3 us -> none  [the longest x6 20 us: last_state(): jnp.einsum('nr,nc->rc', right_wide[position], solved, precision=HIGHEST_P...]
    pallas_call x0 -> x1, Pallas kernels: none -> 60.1 us  [shards(): pl.pallas_call(kernel, out_shape=(jax.ShapeDtypeStruct((1024, 512), BF16)...]
    another operation x10 -> x0, other arithmetic: 28.8 us -> none  [the longest x4 12.6 us: lower_inverse(): gram_lower = jnp.linalg.cholesky(gram_matrix)]
    ppermute x3 -> x0, starting transfers between devices: 10.7 us -> none  [from_behind(): return lax.ppermute(block, axis, route)]
    while x14 -> x0, local copies, waits for them, and re-layouts: 7.89 us -> none  [the longest x2 7.87 us: shards(): lax.fori_loop(0, lax.axis_size('row') - 1, relay_section, carry_in)]
    ppermute x3 -> x0, waiting for transfers between devices: 5.77 us -> none  [from_behind(): return lax.ppermute(block, axis, route)]
  transfers between devices with their start and end apart: 5 -> 0, of which waited for: 5 -> 0; matrix products, arithmetic and copies ran while one was open for 4% -> 0% of each run, Pallas kernels for 0% -> 0%
where the time goes in v1:
time: 66.7 us; the launch traced here: 66.5 us
  Pallas kernels  60.1 us (90%)
  local copies, waits for them, and re-layouts  5.76 us (9%)
    pallas_call x1, Pallas kernels, shards(): pl.pallas_call(kernel, out_shape=(jax.ShapeDtypeStruct((1024, 512), BF16)...  60.1 us
    unnamed x8, local copies, waits for them, and re-layouts  5.76 us

profile of v1, /device:TPU:1, one launch (start us, length us, event | category | flops | bytes accessed | tf_op | source)
XLA Modules:
  0.0 66.5 jit_solution(11372849187240981306)
XLA Ops:
  0.6 60.1 %panel_update.1 = (bf16[1024,512]{1,0:T(8,128)(2,1)}, f32[2,16,64]{2,1,0:T(8,128)}, bf16[2,1024,512]{2,1,0:T(8,128)(2,1)}, f32[2,64,512]{2,1,0:T(8,128)}) custom-call(bf16[128,1024]{1,0:T(8,128)(2,1)} %bitcast.25, bf16[128,1024]{1,0:T(8,128)(2,1)} %bitcast.26, bf16[64,1024]{1,0:T(8,128)(2,1)} %bitcast.31, bf16[64,1024]{1,0:T(8,128)(2,1)} %bitcast.32, ...), custom_call_target="tpu_custom_call" | custom-call | tf_op jit(solution)/shard_map/panel_update/pallas_call | solution.py:614
  60.8 0.0 copy-start
  60.8 2.4 %copy.22 = bf16[1024,512]{1,0:T(8,128)(2,1)} copy(bf16[1024,512]{1,0:T(8,128)(2,1)} %get-tuple-element.8) | data formatting | bytes 2097152
  63.2 1.3 %copy.23 = f32[2,16,64]{2,1,0:T(8,128)} copy(f32[2,16,64]{2,1,0:T(8,128)} %get-tuple-element.9) | data formatting | bytes 16384
  64.5 0.0 copy-done
  64.5 0.0 copy-start.1
  64.5 1.3 %copy.24 = bf16[2,1024,512]{2,1,0:T(8,128)(2,1)} copy(bf16[2,1024,512]{2,1,0:T(8,128)(2,1)S(1)} %copy-done) | data formatting | bytes 4194304
  65.8 0.0 copy-done.1
  65.8 0.7 %copy.25 = f32[2,64,512]{2,1,0:T(8,128)} copy(f32[2,64,512]{2,1,0:T(8,128)S(1)} %copy-done.1) | data formatting | bytes 524288
Async XLA Ops:
  60.8 3.7 %copy-start = (bf16[2,1024,512]{2,1,0:T(8,128)(2,1)S(1)}, bf16[2,1024,512]{2,1,0:T(8,128)(2,1)}, u32[]{:S(2)}) copy-start(bf16[2,1024,512]{2,1,0:T(8,128)(2,1)} %get-tuple-element.10) | copy-start | bytes 6291460
  64.5 1.3 %copy-start.1 = (f32[2,64,512]{2,1,0:T(8,128)S(1)}, f32[2,64,512]{2,1,0:T(8,128)}, u32[]{:S(2)}) copy-start(f32[2,64,512]{2,1,0:T(8,128)} %get-tuple-element.11) | copy-start | bytes 786436

commit v2 on v1

v2 whole, which is shorter than its diff:
```python
import jax
import jax.numpy as jnp
from jax import lax
from jax.experimental import pallas as pl
from jax.experimental.pallas import tpu as pltpu
from jax.sharding import PartitionSpec as P

F32 = jnp.float32
BF16 = jnp.bfloat16
HIGHEST = lax.Precision.HIGHEST
MESH = pl.DeviceIdType.MESH
NY, NZ, NX = 4, 8, 4
BLK = 256
KERNEL_VMEM = 48 * 1024 * 1024
CLOSING_VMEM = 8 * 1024 * 1024


def nn(a, b):
    return jnp.dot(a, b, preferred_element_type=F32)


def nt(a, b):
    return lax.dot_general(a, b, (((1,), (1,)), ((), ())), preferred_element_type=F32)


def tn(a, b):
    return lax.dot_general(a, b, (((0,), (0,)), ((), ())), preferred_element_type=F32)


def nn_full(a, b):
    return jnp.dot(a, b, precision=HIGHEST, preferred_element_type=F32)


def nt_full(a, b):
    return lax.dot_general(
        a, b, (((1,), (1,)), ((), ())), precision=HIGHEST, preferred_element_type=F32
    )


def high_low(a):
    high = a.astype(BF16)
    return high, (a - high.astype(F32)).astype(BF16)


def stacked_parts(a):
    return jnp.concatenate(high_low(a), axis=0)


def joined_rows(a):
    half = a.shape[0] // 2
    return a[:half] + a[half:]


def distance(k):
    return 4 + lax.div(k + 1, 2) * (1 - 2 * lax.rem(k, 2))


def kernel(
    tl_h, tr_h, rl_h, rr_h, sk_h, pl_h, pr_h, pi_h, bi_h, ll_h, lr_h, prhs_h, brhs_h, carry_h,
    ps, srout, l0, xx, right, states,
    tl, tr, rl, rr, sk, plt, prt, pi, bi, ll, lr, prhs, red, carry,
    redlow, pulled, pulledlow, rl2, coup, vhl, pchl, ms, a0,
    terms1, core1, sum1, yin1, ysum1, zin1, full1,
    terms2, core2, sum2, yin2, ysum2, zin2, full2, zfull,
    yfull, yhl, qh, chol, bt, ey, es,
    xa_own, xn_own, xa, xn, xz_own, xz, cps, early,
    load_sem, c_recv, y_recv, z_recv, rs_send,
    gz_recv, gy_recv, gc_recv, ag_send, x_send, x_recv,
):
    me = lax.axis_index("col")
    x = lax.axis_index("row")
    c = lax.rem(me, 2)
    z = lax.rem(lax.div(me, 2), NZ)
    y = lax.div(me, 2 * NZ)

    def at_core():
        return {"col": (y * NZ + z) * 2 + (1 - c)}

    def at_y(dy):
        return {"col": (lax.rem(y + dy, NY) * NZ + z) * 2 + c}

    def at_z(d):
        return {"col": (y * NZ + lax.rem(z + d, NZ)) * 2 + c}

    def at_x(d):
        return {"row": lax.rem(x + d, NX)}

    loads = [
        pltpu.make_async_copy(src, dst, load_sem.at[i])
        for i, (src, dst) in enumerate(
            [
                (sk_h, sk), (rl_h, rl), (rr_h, rr), (tr_h, tr), (tl_h, tl),
                (pi_h, pi), (prhs_h, prhs), (lr_h, lr), (bi_h, bi), (ll_h, ll),
                (pr_h, prt), (pl_h, plt), (brhs_h, red), (carry_h, carry),
            ]
        )
    ]
    for i in range(5):
        loads[i].start()

    barrier = pltpu.get_barrier_semaphore()
    peers = [at_core()]
    peers += [at_y(d) for d in range(1, NY)]
    peers += [at_z(d) for d in range(1, NZ)]
    peers += [at_x(d) for d in range(1, NX)]
    for peer in peers:
        pl.semaphore_signal(barrier, inc=1, device_id=peer, device_id_type=MESH)

    def remote(src, dst, send, recv, device):
        return pltpu.make_async_remote_copy(
            src_ref=src, dst_ref=dst, send_sem=send, recv_sem=recv,
            device_id=device, device_id_type=MESH,
        )

    def loop(first, last, body):
        def step(k, carried):
            body(k)
            return carried

        lax.fori_loop(first, last, step, 0)

    def reduce_scatter(s, terms, core, total, yin, ysum, zin):
        send = rs_send.at[s]

        def group(k):
            return lax.rem(z + distance(k), NZ) * NY

        def core_copy(k):
            at = group(k)
            return remote(
                terms.at[pl.ds((1 - c) * 32 + at, NY)], core.at[pl.ds(at, NY)],
                send, c_recv.at[s, k], at_core(),
            )

        def y_copy(k, dy):
            return remote(
                total.at[group(k) + lax.rem(y + dy, NY)], yin.at[k, dy - 1],
                send, y_recv.at[s, k], at_y(dy),
            )

        def z_copy(k):
            return remote(ysum.at[k], zin.at[k], send, z_recv.at[s], at_z(distance(k)))

        def send_core():
            loop(0, NZ, lambda k: core_copy(k).start())

        def fold_core(first, last):
            def body(k):
                core_copy(k).wait_recv()
                at = group(k)
                total[pl.ds(at, NY)] = terms[pl.ds(c * 32 + at, NY)] + core[pl.ds(at, NY)]
                for dy in (2, 1, 3):
                    y_copy(k, dy).start()

            loop(first, last, body)

        def y_total(k):
            remote(
                yin.at[k], yin.at[k], send, y_recv.at[s, k], at_y(1)
            ).wait_recv()
            ysum[k] = (total[group(k) + y] + yin[k, 0]) + (yin[k, 1] + yin[k, 2])

        def fold_y():
            def body(k):
                y_total(k)
                z_copy(k).start()

            loop(0, NZ - 1, body)
            y_total(NZ - 1)

        def fold_z():
            remote(zin, zin, send, z_recv.at[s], at_z(1)).wait_recv()
            block = ysum[NZ - 1]
            for k in range(NZ - 1):
                block = block + zin[k]
            return block

        def finish():
            sent = terms.at[pl.ds(0, 63)]
            remote(sent, sent, send, z_recv.at[s], at_z(1)).wait_send()

        return send_core, fold_core, fold_y, fold_z, finish

    def all_gather(s, full):
        send = ag_send.at[s]

        def spot(k, side):
            return (c * NZ + lax.rem(z - distance(k) + NZ, NZ)) * NY + lax.rem(y + side, NY)

        def block_copy(at, recv, device):
            block = full.at[at]
            return remote(block, block, send, recv, device)

        def z_copy(k):
            return block_copy((c * NZ + z) * NY + y, gz_recv.at[s, k], at_z(distance(k)))

        def z_wait(k):
            block_copy(spot(k, 0), gz_recv.at[s, k], at_z(distance(k))).wait_recv()

        def spread_y(k):
            for dy in (2, 1, 3):
                block_copy(spot(k, 0), gy_recv.at[s, k], at_y(dy)).start()

        def groups(side, first, count):
            return full.at[pl.ds(((side * NZ) + first) * NY, count * NY)]

        def core_copy(k):
            group = groups(c, lax.rem(z - distance(k) + NZ, NZ), 1)
            return remote(group, group, send, gc_recv.at[s], at_core())

        def send_z():
            loop(0, NZ - 1, lambda k: z_copy(k).start())
            spread_y(NZ - 1)

        def down(first, last, body):
            loop(0, first - last + 1, lambda i: body(first - i))

        def pass_y(first, last):
            def body(k):
                z_wait(k)
                spread_y(k)

            down(first, last, body)

        def pass_core():
            def body(k):
                three = full.at[pl.ds(0, 3)]
                remote(three, three, send, gy_recv.at[s, k], at_y(1)).wait_recv()
                core_copy(k).start()

            down(NZ - 1, 0, body)

        def arrive():
            half = groups(1 - c, 0, NZ)
            remote(half, half, send, gc_recv.at[s], at_core()).wait_recv()

        def finish():
            sent = full.at[pl.ds(0, 63)]
            remote(sent, sent, send, gc_recv.at[s], at_core()).wait_send()

        return send_z, pass_y, pass_core, arrive, finish

    def x_copy(kind, d):
        src = (xa_own, xn_own, xz_own)[kind]
        dst = (xa, xn, xz)[kind].at[d - 1]
        return remote(src, dst, x_send.at[kind], x_recv.at[kind], at_x(d))

    def x_all(kind):
        dst = (xa, xn, xz)[kind]
        return remote(dst, dst, x_send.at[kind], x_recv.at[kind], at_x(1))

    rs1 = reduce_scatter(0, terms1, core1, sum1, yin1, ysum1, zin1)
    ag1 = all_gather(0, full1)
    rs2 = reduce_scatter(1, terms2, core2, sum2, yin2, ysum2, zin2)
    ag2 = all_gather(1, full2)
    ag3 = all_gather(2, zfull)
    home = (c * NZ + z) * NY + y

    def pivot_rows(m):
        top = (m + 1) * BLK
        block = nn(pi[m * BLK : top, :top], prhs[:top, :])
        ps[m * BLK : top, :] = block.astype(BF16)

    def pulled_rows(m):
        low, top = m * BLK, (m + 1) * BLK
        high, rest = high_low(tn(pi[low:, low:top], ps[low:, :]))
        pulled[low:top, :] = high
        pulledlow[low:top, :] = rest

    def link_inverse(b, m):
        low, top = m * BLK, (m + 1) * BLK
        block = nn(lr[b * 64 : (b + 1) * 64, low:], bi[b, low:, low:top])
        vhl[b, :, low:top] = stacked_parts(block)

    def panel_coeffs():
        coeffs = nn(prt[...], pulled[...]) + nn(prt[...], pulledlow[...])
        for b in range(2):
            pchl[b] = stacked_parts(coeffs[b * 64 : (b + 1) * 64])

    def reduce_rows(b, m):
        low, top = m * BLK, (m + 1) * BLK
        left = plt[b * 64 : (b + 1) * 64, low:top]
        term = tn(jnp.concatenate([left, left], axis=0), pchl[b])
        high, rest = high_low(red[b, low:top, :].astype(F32) - term)
        red[b, low:top, :] = high
        redlow[b, low:top, :] = rest

    def local_rows(b, m):
        low, top = m * BLK, (m + 1) * BLK
        own = bi[b, low:top, :top]
        l0[b, low:top, :] = nn(own, red[b, :top, :]) + nn(own, redlow[b, :top, :])

    def chain_terms():
        for b in range(2):
            ms[b] = joined_rows(nt(vhl[b], ll[b * 64 : (b + 1) * 64, :]))
            a0[b] = joined_rows(nn(vhl[b], red[b]) + nn(vhl[b], redlow[b]))
        through = nn_full(ms[1], ms[0])
        xn_own[...] = through
        first = jnp.where(x == 0, 1.0, 0.0).astype(F32)
        xa_own[...] = (
            a0[1] - nn_full(ms[1], a0[0]) + first * nn_full(through, carry[...])
        )
        for d in range(1, NX):
            x_copy(1, d).start()
            x_copy(0, d).start()

    def chain_start():
        x_all(1).wait_recv()
        x_all(0).wait_recv()
        flag = [jnp.where(x >= d, 1.0, 0.0).astype(F32) for d in range(NX)]
        two = flag[2] * xn[0]
        three = flag[3] * nn_full(xn[0], xn[1])
        cps[0, :64, :] = two
        cps[1, :64, :] = three
        cps[0, 64:, :] = jnp.zeros((64, 64), F32)
        cps[1, 64:, :] = jnp.zeros((64, 64), F32)
        early[...] = (
            (1.0 - flag[1]) * carry[...]
            + flag[1] * xa[0]
            + nn_full(two, xa[1])
            + nn_full(three, xa[2])
        )

    rows_i = lax.broadcasted_iota(jnp.int32, (128, 128), 0)
    cols_i = lax.broadcasted_iota(jnp.int32, (128, 128), 1)

    def gram():
        crosses = []
        for b in range(2):
            high, low = yhl[b, :64, :], yhl[b, 64:, :]
            square = nt(high, high) + (nt(high, low) + nt(low, high))
            eye = jnp.where(
                lax.broadcasted_iota(jnp.int32, (64, 64), 0)
                == lax.broadcasted_iota(jnp.int32, (64, 64), 1),
                1.0,
                0.0,
            ).astype(F32)
            pair = [square, eye] if b == 0 else [eye, square]
            chol[b * 64 : (b + 1) * 64, :] = jnp.concatenate(pair, axis=1)
            cross = joined_rows(nt(vhl[b], yhl[b]))
            crosses.append(cross[:, :64] + cross[:, 64:])
        ey[...] = jnp.concatenate(crosses, axis=1)

    def eliminate(first, last):
        work = [chol[b * 64 : (b + 1) * 64, :] for b in range(2)]
        start = (first // 8) * 8
        for b in range(2):
            work[b] = work[b][start:]
        height = 64 - start
        row_id = lax.broadcasted_iota(jnp.int32, (height, 128), 0) + start
        for k in range(first, last, 4):
            at = k - start
            for b in range(2):
                body = work[b]
                lane = k + 64 * b
                columns = [
                    jnp.broadcast_to(body[:, lane + j : lane + j + 1], (height, 128))
                    for j in range(4)
                ]
                rows = [body[at + j : at + j + 1, :] for j in range(4)]
                for j in range(4):
                    inverse = 1.0 / columns[j][at + j : at + j + 1, :]
                    pivot_row = rows[j] * inverse
                    below = jnp.where(row_id > k + j, columns[j], 0.0)
                    for i in range(j + 1, 4):
                        scale = columns[i][at + j : at + j + 1, :] * inverse
                        columns[i] = columns[i] - below * scale
                        rows[i] = rows[i] - columns[j][at + i : at + i + 1, :] * pivot_row
                    body = body - below * pivot_row
                work[b] = body
        for b in range(2):
            chol[b * 64 + start : (b + 1) * 64, :] = work[b]

    def factors():
        full = chol[...]
        pivots = jnp.sum(jnp.where(rows_i == cols_i, full, 0.0), axis=1, keepdims=True)
        scaled = full * lax.rsqrt(pivots)
        moved = pltpu.roll(scaled, 64, 1)
        same = (rows_i < 64) == (cols_i < 64)
        inverse = jnp.where(same, moved, 0.0)
        bt[:128, :] = inverse
        effect = nt_full(ey[...], inverse)
        es[...] = effect
        outward = jnp.concatenate([-nn_full(ms[1], effect[:, :64]), effect[:, 64:]], axis=1)
        bt[128:192, :] = nn_full(outward, inverse)
        bt[192:, :] = jnp.zeros((64, 128), F32)

    def panel_basis():
        yt = jnp.concatenate([yfull[0], yfull[1]], axis=0)
        qh[...] = nn_full(bt[:128, :], yt).astype(BF16)

    def response_rows(b, m):
        low, top = m * BLK, (m + 1) * BLK
        both = jnp.concatenate(
            [qh[b * 64 : (b + 1) * 64, :top], ll[b * 64 : (b + 1) * 64, :top]], axis=0
        )
        block = nt(bi[b, low:top, :top], both).astype(BF16)
        xx[b, low:top, :128] = block
        xx[b, low:top, 128:] = block

    for i in range(4):
        loads[i].wait()
    for i in range(5, 14):
        loads[i].start()
    probe_t = nt(sk[...], rl[...])
    core_t = nn_full(probe_t, nt(rr[...], tr[...]))
    loads[4].wait()
    for b in range(2):
        own = tl[b * 64 : (b + 1) * 64, :]
        parts = jnp.concatenate(high_low(core_t[:, b * 64 : (b + 1) * 64]), axis=1)
        block = nn(parts, jnp.concatenate([own, own], axis=0))
        for t in range(8):
            at = (2 * t + b) * 4
            terms1[at : at + 4] = block[:, t * 128 : (t + 1) * 128].reshape(4, 16, 128)
    pl.semaphore_wait(barrier, len(peers))
    rs1[0]()
    rs1[1](0, 4)
    wide = rl[...].astype(F32)
    rl2[...] = jnp.concatenate([wide, wide], axis=0).T.astype(BF16)
    coup[...] = nt(tr[...], rr[...])
    loads[5].wait()
    loads[6].wait()
    pivot_rows(0)
    rs1[1](4, NZ)
    for m in range(1, 4):
        pivot_rows(m)
    rs1[2]()
    for m in range(4):
        pulled_rows(m)
    loads[10].wait()
    panel_coeffs()
    loads[7].wait()
    loads[8].wait()
    for b in range(2):
        for m in range(4):
            link_inverse(b, m)
    loads[11].wait()
    loads[12].wait()
    full1[home] = rs1[3]()
    ag1[0]()
    for b in range(2):
        for m in range(4):
            reduce_rows(b, m)
    loads[9].wait()
    loads[13].wait()
    ag1[1](6, 3)
    chain_terms()
    ag1[1](2, 0)
    for m in range(3):
        local_rows(0, m)
    ag1[2]()
    ag1[3]()

    for b in range(2):
        yt = jnp.concatenate(
            [full1[(2 * t + b) * 4 : (2 * t + b) * 4 + 4].reshape(64, 128) for t in range(8)], axis=1
        )
        yfull[b] = yt
        yhl[b] = stacked_parts(yt)
    middles = []
    for b in range(2):
        projected_t = joined_rows(nt(yhl[b], tl[b * 64 : (b + 1) * 64, :]))
        middles.append(nn_full(projected_t, coup[b * 64 : (b + 1) * 64, :]))
    middle_t = jnp.concatenate(middles, axis=0)
    terms2[...] = nt(rl2[...], jnp.concatenate(high_low(middle_t), axis=1)).reshape(64, 16, 128)
    rs2[0]()
    rs2[1](0, 4)
    gram()
    rs2[1](4, NZ)
    for first in range(0, 32, 8):
        eliminate(first, first + 8)
    rs2[2]()
    for first in range(32, 64, 8):
        eliminate(first, first + 8)
    factors()
    shard = nt_full(rs2[3](), bt[...])
    xz_own[...] = shard[:, 128:]
    for d in range(1, NX):
        x_copy(2, d).start()
    full2[home] = shard[:, :128]
    ag2[0]()
    chain_start()
    panel_basis()
    ag2[1](6, 3)
    x_all(2).wait_recv()
    near_flag = jnp.where(x >= 1, 1.0, 0.0).astype(F32)
    onward = (
        near_flag * xz[0] + nt_full(xz[1][:, :64], cps[0]) + nt_full(xz[2][:, :64], cps[1])
    )
    zfull[home] = jnp.concatenate([onward[:8, :64], onward[8:, :64]], axis=1)
    ag3[0]()
    ag2[1](2, 0)
    local_rows(0, 3)
    local_rows(1, 0)
    ag3[1](6, 0)
    for m in range(1, 4):
        local_rows(1, m)
    ag2[2]()
    for b in range(2):
        for m in range(4):
            response_rows(b, m)
    ag2[3]()
    mine = full2[me]
    srout[0] = mine[:, :64]
    srout[1] = mine[:, 64:]
    high, rest = high_low(full2[...].reshape(1024, 128))
    coeffs = tn(high, pulled[...]) + (tn(rest, pulled[...]) + tn(high, pulledlow[...]))
    for b in range(2):
        own = coeffs[b * 64 : (b + 1) * 64]
        high, rest = high_low(own)
        right[b, :64, :] = high
        right[b, 128:192, :] = rest
        states[b] = a0[b] + nn_full(es[:, b * 64 : (b + 1) * 64], own)
    ag3[2]()
    ag3[3]()

    packed = zfull[...]
    onward = jnp.concatenate([packed[:, :, :64], packed[:, :, 64:]], axis=1).reshape(1024, 64)
    shift = joined_rows(tn(jnp.concatenate(high_low(onward), axis=1), pulled[...]))
    prior = early[...] + shift
    for b in range(2):
        high, rest = high_low(-prior)
        right[b, 64:128, :] = high
        right[b, 192:, :] = rest
        prior = states[b] - nn_full(ms[b], prior)
        states[b] = prior

    for phase in (rs1, rs2, ag1, ag2, ag3):
        phase[4]()
    for kind in range(3):
        x_all(kind).wait_send()


def closing_kernel(ps, srout, l0, xx, right, states, ps_o, sr_o, bs_o, ls_o, sol, sem, sol_sem):
    copies = [
        pltpu.make_async_copy(src, dst, sem.at[i])
        for i, (src, dst) in enumerate([(ps, ps_o), (states, ls_o), (srout, sr_o)])
    ]
    for copy in copies:
        copy.start()
    for b in range(2):
        for m in range(4):
            low, top = m * BLK, (m + 1) * BLK
            sol[b, low:top, :] = (l0[b, low:top, :] + nn(xx[b, low:top, :], right[b])).astype(BF16)
            copy = pltpu.make_async_copy(
                sol.at[b, pl.ds(low, BLK)], bs_o.at[b, pl.ds(low, BLK)], sol_sem.at[4 * b + m]
            )
            copy.start()
            copies.append(copy)
    for copy in copies:
        copy.wait()


def flipped(array):
    return jnp.swapaxes(array, -1, -2)


def shards(
    tile_left, tile_right, row_left, row_right, sketch, panel_left, panel_right,
    pivot_inverse, band_inverse, link_left, link_right, pivot_rhs, band_rhs, carry_in,
):
    args = (
        flipped(tile_left).reshape(128, 1024),
        flipped(tile_right).reshape(128, 1024),
        flipped(row_left).reshape(64, 1024),
        flipped(row_right).reshape(64, 1024),
        flipped(sketch),
        flipped(panel_left).reshape(128, 1024),
        flipped(panel_right).reshape(128, 1024),
        pivot_inverse,
        band_inverse,
        flipped(link_left).reshape(128, 1024),
        flipped(link_right).reshape(128, 1024),
        pivot_rhs,
        band_rhs,
        carry_in,
    )
    vm = pltpu.VMEM
    comm = (64, 16, 128)

    def comm_scratch():
        return [
            vm(comm, F32), vm((32, 16, 128), F32), vm((32, 16, 128), F32),
            vm((8, 3, 16, 128), F32), vm((8, 16, 128), F32), vm((7, 16, 128), F32), vm(comm, F32),
        ]

    scratch = [
        vm((128, 1024), BF16), vm((128, 1024), BF16), vm((64, 1024), BF16), vm((64, 1024), BF16),
        vm((64, 1024), BF16), vm((128, 1024), BF16), vm((128, 1024), BF16), vm((1024, 1024), BF16),
        vm((2, 1024, 1024), BF16), vm((128, 1024), BF16), vm((128, 1024), BF16),
        vm((1024, 512), BF16), vm((2, 1024, 512), BF16), vm((64, 512), F32),
        vm((2, 1024, 512), BF16), vm((1024, 512), BF16), vm((1024, 512), BF16),
        vm((1024, 128), BF16), vm((128, 64), F32),
        vm((2, 128, 1024), BF16), vm((2, 128, 512), BF16),
        vm((2, 64, 64), F32), vm((2, 64, 512), F32),
        *comm_scratch(),
        *comm_scratch(), vm((64, 8, 128), F32),
        vm((2, 64, 1024), F32), vm((2, 128, 1024), BF16), vm((128, 1024), BF16),
        vm((128, 128), F32), vm((256, 128), F32), vm((64, 128), F32), vm((64, 128), F32),
        vm((64, 512), F32), vm((64, 64), F32), vm((3, 64, 512), F32), vm((3, 64, 64), F32),
        vm((16, 128), F32), vm((3, 16, 128), F32), vm((2, 128, 64), F32), vm((64, 512), F32),
    ]
    dma = pltpu.SemaphoreType.DMA
    sems = [
        dma((14,)), dma((2, 8)), dma((2, 8)), dma((2,)), dma((2,)),
        dma((3, 7)), dma((3, 8)), dma((3,)), dma((3,)), dma((3,)), dma((3,)),
    ]
    anywhere = pl.BlockSpec(memory_space=pl.ANY)
    inside = pl.BlockSpec(memory_space=pltpu.VMEM)
    held = pl.pallas_call(
        kernel,
        out_shape=(
            vm((1024, 512), BF16),
            vm((2, 16, 64), F32),
            vm((2, 1024, 512), F32),
            vm((2, 1024, 256), BF16),
            vm((2, 256, 512), BF16),
            vm((2, 64, 512), F32),
        ),
        in_specs=[anywhere] * 14,
        out_specs=(inside,) * 6,
        scratch_shapes=scratch + sems,
        compiler_params=pltpu.CompilerParams(
            collective_id=0, has_side_effects=True, vmem_limit_bytes=KERNEL_VMEM
        ),
        name="panel_update",
    )(*args)
    return pl.pallas_call(
        closing_kernel,
        out_shape=(
            jax.ShapeDtypeStruct((1024, 512), BF16),
            jax.ShapeDtypeStruct((2, 16, 64), F32),
            jax.ShapeDtypeStruct((2, 1024, 512), BF16),
            jax.ShapeDtypeStruct((2, 64, 512), F32),
        ),
        in_specs=[inside] * 6,
        out_specs=(anywhere,) * 4,
        scratch_shapes=[vm((2, 1024, 512), BF16), dma((3,)), dma((8,))],
        compiler_params=pltpu.CompilerParams(vmem_limit_bytes=CLOSING_VMEM),
        name="solutions",
    )(*held)


def solution(mesh):
    return jax.shard_map(
        shards,
        mesh=mesh,
        in_specs=(
            P("col", "row", None, None),
            P("col", "row", None, None),
            P("col", None, None),
            P("col", None, None),
            P(),
            P("row", None, None),
            P("row", None, None),
            P(),
            P("row", None, None),
            P("row", None, None),
            P("row", None, None),
            P(None, "col"),
            P("row", None, "col"),
            P(None, "col"),
        ),
        out_specs=(
            P(None, "col"),
            P("row", "col", None),
            P("row", None, "col"),
            P("row", None, "col"),
        ),
        check_vma=False,
    )
```

time: 66.7 us -> 58.5 us (0.88)
  local copies, waits for them, and re-layouts: 5.76 us -> 0 us
  Pallas kernels: 60.1 us -> 57.8 us
    unnamed x8 -> x0, local copies, waits for them, and re-layouts: 5.76 us -> none
    pallas_call x1 -> x2, Pallas kernels: 60.1 us -> 57.8 us  [the longest x1 55.9 us: shards(): pl.pallas_call(kernel, out_shape=(vm((1024, 512), BF16), vm((2, 16, 64),...]
where the time goes in v2:
time: 58.5 us; the launch traced here: 58.4 us
  Pallas kernels  57.8 us (99%)
  between operations  0.64 us (1%)
    pallas_call x1, Pallas kernels, shards(): pl.pallas_call(kernel, out_shape=(vm((1024, 512), BF16), vm((2, 16, 64),...  55.9 us
    pallas_call x1, Pallas kernels, shards(): pl.pallas_call(closing_kernel, out_shape=(jax.ShapeDtypeStruct((1024, 512...  1.85 us

profile of v2, /device:TPU:1, one launch (start us, length us, event | category | flops | bytes accessed | tf_op | source)
XLA Modules:
  0.0 58.4 jit_solution(11131915739320374500)
XLA Ops:
  0.6 55.9 %panel_update.1 = (bf16[1024,512]{1,0:T(8,128)(2,1)S(1)}, f32[2,16,64]{2,1,0:T(8,128)S(1)}, f32[2,1024,512]{2,1,0:T(8,128)S(1)}, bf16[2,1024,256]{2,1,0:T(8,128)...) custom-call(bf16[128,1024]{1,0:T(8,128)(2,1)} %bitcast.25, bf16[128,1024]{1,0:T(8,128)(2,1)} %bitcast.26, ...), custom_call_target="tpu_custom_call" | custom-call | tf_op jit(solution)/shard_map/panel_update/pallas_call | solution.py:610
  56.6 1.9 %solutions.1 = (bf16[1024,512]{1,0:T(8,128)(2,1)}, f32[2,16,64]{2,1,0:T(8,128)}, bf16[2,1024,512]{2,1,0:T(8,128)(2,1)}, f32[2,64,512]{2,1,0:T(8,128)}) custom-call(bf16[1024,512]{1,0:T(8,128)(2,1)S(1)} %get-tuple-element.10.ps, f32[2,16,64]{2,1,0:T(8,128)S(1)} %get-tuple-element.11.srout, f32[2,1024,512]{2,1,0:T(8,128)S(1)} %get-tuple-element.12.l0, ...), custom_call_target="tpu_custom_call" | custom-call | tf_op jit(solution)/shard_map/solutions/pallas_call | solution.py:628
